TPU v7x, 32 devices: a whole 2x2x4 slice. The times are simulated.
32 devices in a mesh: dp: 8 (over y, x, core), mp: 4 (over z).
Axes of the slice: x: 2, y: 2, z: 4, core: 2. Of those that a mesh axis runs over, the one named last changes fastest.
Arguments:
- hidden_states: bfloat16 [4096, 4096], P('dp', 'mp'), may hold values from -40 to 40
- norm_gain: float32 [1, 4096], replicated, may hold values from 0.1 to 1.9
- query_weight: bfloat16 [1, 4096, 4096], P(None, 'dp', 'mp'), may hold values from -0.01171875 to 0.01171875
- keyvalue_weight: bfloat16 [1, 4096, 2, 4096], P(None, 'dp', None, 'mp'), may hold values from -0.09375 to 0.09375
- output_weight: bfloat16 [1, 4096, 4096], P(None, 'dp', 'mp'), may hold values from -0.09375 to 0.09375
- position_bias: float32 [1, 32, 64], P(None, None, 'mp'), may hold values from -8 to 250
- lengths: int32 [32], P('dp'), may hold values from 16 to 128
Outputs:
- layer_output: bfloat16 [4096, 4096], P('dp', 'mp')
All inputs are finite; a program needn't handle non-finite values.
Results may differ from a plain program's by a relative error of at most 0.006.
Values may be sent and summed in bfloat16 or wider, within the bound.
No kernel may reach another device: no remote copies, remote signals or barrier semaphores. Data moves between devices by JAX's collectives and lax.ppermute only.
A program may use at most 128 MiB of HBM per device.

v0:
```python
import jax
import jax.numpy as jnp
import numpy as np
from jax import lax
from jax.sharding import PartitionSpec as P

DH = 64
BUCKETS = 32
DIST = 128
LEN = 128
epsilon = 1e-06


def bucket_table():
    half_count = BUCKETS // 2
    exact_count = half_count // 2
    positions = np.arange(LEN)
    relative = positions[None, :] - positions[:, None]
    distance = np.abs(relative)
    scaled = (
        np.log(np.maximum(distance, 1) / exact_count)
        / np.log(DIST / exact_count)
        * (half_count - exact_count)
    )
    far_bucket = np.minimum(exact_count + np.floor(scaled + 1e-09).astype(np.int32), half_count - 1)
    near_bucket = np.where(distance < exact_count, distance, far_bucket)
    return (near_bucket + np.where(relative > 0, half_count, 0)).astype(np.int32)


def normed_rows(hidden, gain_row):
    values = hidden.astype(jnp.float32)
    mean_square = jnp.mean(values * values, axis=-1, keepdims=True)
    return (values * lax.rsqrt(mean_square + epsilon) * gain_row).astype(jnp.bfloat16)


def add_projections(query_acc, pair_acc, normed, query_piece, pair_piece):
    query_acc = jnp.dot(normed, query_piece, preferred_element_type=jnp.float32)
    pair_acc = jnp.einsum("td,dcf->ctf", normed, pair_piece, preferred_element_type=jnp.float32)
    return (query_acc, pair_acc)


def local(
    hidden_states, norm_gain, query_weight, keyvalue_weight, output_weight, position_bias, lengths
):
    captions = lengths.shape[0]
    tokens_here = hidden_states.shape[0]
    heads_here = position_bias.shape[2]
    inner_here = heads_here * DH
    bucket_onehot = jnp.asarray(
        (bucket_table()[:, :, None] == np.arange(BUCKETS)[None, None, :]).astype(np.float32)
    )
    visible = jnp.arange(LEN)[None, :] < lengths[:, None]
    hidden = hidden_states
    gathered = lax.all_gather(hidden, "mp", axis=1, tiled=True)
    normed = normed_rows(gathered, norm_gain[0])
    zero_queries = jnp.zeros((tokens_here, inner_here), jnp.float32)
    zero_pairs = jnp.zeros((2, tokens_here, inner_here), jnp.float32)
    query_rows = query_weight[0]
    pair_rows = keyvalue_weight[0]
    out_rows = output_weight[0]
    query_acc, pair_acc = add_projections(
        zero_queries,
        zero_pairs,
        normed,
        lax.all_gather(query_rows, "dp", axis=0, tiled=True),
        lax.all_gather(pair_rows, "dp", axis=0, tiled=True),
    )
    queries = query_acc.astype(jnp.bfloat16).reshape(captions, LEN, heads_here, DH)
    key_rows = pair_acc[0].astype(jnp.bfloat16).reshape(captions, LEN, heads_here, DH)
    value_rows = pair_acc[1].astype(jnp.bfloat16).reshape(captions, LEN, heads_here, DH)
    position_terms = jnp.einsum(
        "qkb,bh->hqk", bucket_onehot, position_bias[0], precision=lax.Precision.HIGHEST
    )
    scores = (
        jnp.einsum("cqhe,ckhe->chqk", queries, key_rows, preferred_element_type=jnp.float32)
        + position_terms[None]
    )
    scores = jnp.where(visible[:, None, None, :], scores, -1e30)
    maxima = jnp.max(scores, axis=-1, keepdims=True)
    raised = jnp.exp(scores - maxima)
    weights = (raised / jnp.sum(raised, axis=-1, keepdims=True)).astype(jnp.bfloat16)
    mixture = jnp.einsum("chqk,ckhe->cqhe", weights, value_rows, preferred_element_type=jnp.float32)
    attended = mixture.astype(jnp.bfloat16).reshape(tokens_here, inner_here)
    partial_out = jnp.einsum(
        "tf,df->td",
        attended,
        lax.all_gather(out_rows, "dp", axis=0, tiled=True),
        preferred_element_type=jnp.float32,
    )
    reduced = lax.psum_scatter(
        partial_out.astype(jnp.bfloat16), "mp", scatter_dimension=1, tiled=True
    ).astype(jnp.float32)
    hidden = (hidden.astype(jnp.float32) + reduced).astype(jnp.bfloat16)
    return hidden


def solution(mesh):
    in_specs = (
        P("dp", "mp"),
        P(),
        P(None, "dp", "mp"),
        P(None, "dp", None, "mp"),
        P(None, "dp", "mp"),
        P(None, None, "mp"),
        P("dp"),
    )
    out_specs = P("dp", "mp")
    return jax.shard_map(local, mesh=mesh, in_specs=in_specs, out_specs=out_specs, check_vma=False)
```

profile of v0, /device:TPU:0, one launch (start us, length us, event | category | flops | bytes accessed | tf_op | source)
XLA Modules:
  0.0 390.5 jit_solution(6013965719425897973)
XLA Ops:
  6.5 0.7 all-gather.8.cloned.1.call-update
  7.3 0.7 all-gather.12.cloned.1.call-update
  8.1 3.5 copy.15
  11.7 0.5 all-gather.14.cloned.1.call-update
  12.3 1.2 convolution_bitcast_fusion
  13.5 1.4 copy.21
  15.0 77.4 %all-gather.8.cloned.1.call-done = bf16[512,4096]{1,0:T(8,128)(2,1)} async-done(((bf16[512,1024]{1,0:T(8,128)(2,1)}), bf16[512,4096]{1,0:T(8,128)(2,1)}) %all-gather.8.cloned.1.call-update) | async-done | bytes 4194320 | tf_op jit(solution)/shard_map/all_gather | solution.py:54
  92.4 3.1 fusion.3
  95.5 51.6 %all-gather.12.cloned.1.call-done = bf16[1,4096,1024]{2,1,0:T(8,128)(2,1)} async-done(((bf16[1,512,1024]{2,1,0:T(8,128)(2,1)}), bf16[1,4096,1024]{2,1,0:T(8,128)(2,1)}) %all-gather.12.cloned.1.call-update) | async-done | bytes 8388624 | tf_op jit(solution)/shard_map/all_gather | solution.py:65
  147.1 9.2 %fusion.27 = bf16[512,1024]{1,0:T(8,128)(2,1)S(1)} fusion(bf16[1,4096,1024]{2,1,0:T(8,128)(2,1)} %all-gather.12.cloned.1.call-done, bf16[512,4096]{1,0:T(8,128)(2,1)} %all-gather.8.cloned.1.call-done, f32[4096]{0:T(1024)S(1)} %bitcast.40, f32[512]{0:T(512)S(1)} %add_rsqrt_fusion), kind=kOutput, calls=%fused_computation.28 | convolution fusion | flops 4303880192 | bytes 13649920 | tf_op jit(solution)/shard_map/dot_general | solution.py:37
  156.3 1.5 reshape.48
  157.8 80.9 %all-gather.10.cloned.1.call-done = bf16[1,4096,2,1024]{3,1,2,0:T(8,128)(2,1)} async-done(((bf16[1,512,2,1024]{3,1,2,0:T(8,128)(2,1)}), bf16[1,4096,2,1024]{3,1,2,0:T(8,128)(2,1)}) %all-gather.10.cloned.1.call-update) | async-done | bytes 16777232 | tf_op jit(solution)/shard_map/all_gather | solution.py:66
  238.7 13.7 %convert_bitcast_fusion = bf16[2,512,1024]{2,1,0:T(8,128)(2,1)S(1)} fusion(bf16[1,4096,2,1024]{3,1,2,0:T(8,128)(2,1)} %all-gather.10.cloned.1.call-done, bf16[512,4096]{1,0:T(8,128)(2,1)} %all-gather.8.cloned.1.call-done, f32[4096]{0:T(1024)S(1)} %bitcast.41, f32[512]{0:T(512)S(1)} %add_rsqrt_fusion), kind=kOutput, calls=%fused_computation.23 | convolution fusion | flops 8599371776 | bytes 23087104 | tf_op jit(solution)/shard_map/td,dcf->ctf/dot_general | solution.py:38
  252.4 1.1 fusion.42
  253.6 4.0 %reshape.49 = bf16[4,128,16,64]{3,2,1,0:T(8,128)(2,1)} reshape(bf16[1,512,1024]{2,1,0:T(8,128)(2,1)} %get-tuple-element.6) | data formatting | bytes 2097152 | tf_op jit(solution)/shard_map/convert_element_type | solution.py:69
  257.6 2.3 reshape.47
  259.9 3.3 fusion.15
  263.2 1.8 fusion.43
  265.0 0.8 fusion.33
  265.8 0.9 copy.24
  266.7 28.1 %all-gather.14.cloned.1.call-done = bf16[1,4096,1024]{2,1,0:T(8,128)(2,1)} async-done(((bf16[1,512,1024]{2,1,0:T(8,128)(2,1)}), bf16[1,4096,1024]{2,1,0:T(8,128)(2,1)}) %all-gather.14.cloned.1.call-update) | async-done | bytes 8388624 | tf_op jit(solution)/shard_map/all_gather | solution.py:87
  294.8 9.6 %fusion.10 = bf16[512,4096]{1,0:T(8,128)(2,1)} fusion(bf16[1,4096,1024]{2,1,0:T(8,128)(2,1)} %all-gather.14.cloned.1.call-done, bf16[128,8,4,128]{3,2,1,0:T(4,128)(2,1)S(1)} %bitcast.39), kind=kOutput, calls=%fused_computation.12 | convolution fusion | flops 4297064448 | bytes 13631488 | tf_op jit(solution)/shard_map/tf,df->td/dot_general | solution.py:84
  304.4 77.0 %reduce-scatter.2.cloned.1.call-done = bf16[512,1024]{1,0:T(8,128)(2,1)} async-done(((bf16[512,4096]{1,0:T(8,128)(2,1)}), bf16[512,1024]{1,0:T(8,128)(2,1)}) %reduce-scatter.2.cloned.1.call-update) | async-done | bytes 1048592 | tf_op jit(solution)/shard_map/reduce_scatter | solution.py:90
  381.3 2.6 add_convert_fusion
  (25 shorter events, 0.3 us)
Async XLA Ops:
  6.5 5.7 %copy-start = (f32[1,32,16]{1,2,0:T(8,128)S(1)}, f32[1,32,16]{1,2,0:T(8,128)}, u32[]{:S(2)}) copy-start(f32[1,32,16]{1,2,0:T(8,128)} %param.13) | copy-start | bytes 6148
  6.5 85.9 %all-gather.8.cloned.1.call-start = ((), (), s32[]{:S(2)}) async-start(), calls=%async_computation.1 | async-start | bytes 5242880 | tf_op jit(solution)/shard_map/all_gather | solution.py:54
  7.3 5.0 %copy-start.3 = (f32[128,128,32]{1,2,0:T(8,128)S(1)}, f32[128,128,32]{1,2,0:T(8,128)}, u32[]{:S(2)}) copy-start(f32[128,128,32]{1,2,0:T(8,128)} %constant.13.clone) | copy-start | bytes 6291460
  7.3 139.8 %all-gather.12.cloned.1.call-start = ((), (), s32[]{:S(2)}) async-start(), calls=%async_computation.4 | async-start | bytes 9437184 | tf_op jit(solution)/shard_map/all_gather | solution.py:65
  8.0 230.7 %all-gather.10.cloned.1.call-start = ((), (), s32[]{:S(2)}) async-start(), calls=%async_computation.3 | async-start | bytes 18874368 | tf_op jit(solution)/shard_map/all_gather | solution.py:66
  11.6 3.3 copy-start.7
  11.6 283.2 %all-gather.14.cloned.1.call-start = ((), (), s32[]{:S(2)}) async-start(), calls=%async_computation.5 | async-start | bytes 9437184 | tf_op jit(solution)/shard_map/all_gather | solution.py:87
  12.2 134.9 %copy-start.6 = (f32[1,4096]{1,0:T(1,128)S(1)}, f32[1,4096]{1,0:T(1,128)}, u32[]{:S(2)}) copy-start(f32[1,4096]{1,0:T(1,128)} %param.9) | copy-start | bytes 49156
  12.2 369.1 %reduce-scatter.2.cloned.1.call-start = ((), (), s32[]{:S(2)}) async-start(), calls=%async_computation.2 | async-start | bytes 5242880 | tf_op jit(solution)/shard_map/reduce_scatter | solution.py:90
  259.9 3.3 copy-start.5
  263.2 1.8 copy-start.4
  294.8 89.2 %copy-start.1 = (f32[1,32,16]{1,2,0:T(8,128)S(1)}, f32[1,32,16]{1,2,0:T(8,128)}, u32[]{:S(2)}) copy-start(f32[1,32,16]{1,2,0:T(8,128)} %param.13) | copy-start | bytes 6148
  304.4 77.0 %copy-start.2 = (bf16[512,1024]{1,0:T(8,128)(2,1)S(1)}, bf16[512,1024]{1,0:T(8,128)(2,1)}, u32[]{:S(2)}) copy-start(bf16[512,1024]{1,0:T(8,128)(2,1)} %param.8) | copy-start | bytes 3145732
Sparse Core Ops, SparseCore 0:
  8.9 83.4 all-gather.7
  94.3 52.7 all-gather.11
  149.0 89.7 all-gather.9
  240.5 54.2 all-gather.13
  304.5 76.7 reduce-scatter.1
where the time goes:
time: 391 us; the launch traced here: 390 us
  waiting for transfers between devices  317 us (81%)
  matrix products  37.7 us (10%)
  local copies, waits for them, and re-layouts  14.9 us (4%)
  between operations  13.2 us (3%)
  other arithmetic  7.56 us (2%)
    all_gather x1, waiting for transfers between devices, local(): lax.all_gather(pair_rows, 'dp', axis=0, tiled=True)  80.9 us
    all_gather x1, waiting for transfers between devices, local(): gathered = lax.all_gather(hidden, 'mp', axis=1, tiled=True)  77.4 us
    reduce_scatter x1, waiting for transfers between devices, local(): lax.psum_scatter(partial_out.astype(jnp.bfloat16), 'mp', scatter_dimensio...  77 us
    all_gather x1, waiting for transfers between devices, local(): lax.all_gather(query_rows, 'dp', axis=0, tiled=True)  51.6 us
    all_gather x1, waiting for transfers between devices, local(): lax.all_gather(out_rows, 'dp', axis=0, tiled=True)  28.1 us
    dot_general x1, matrix products, add_projections(): jnp.einsum('td,dcf->ctf', normed, pair_piece, preferred_element_type=jnp....  13.7 us
    dot_general x1, matrix products, local(): jnp.einsum('tf,df->td', attended, lax.all_gather(out_rows, 'dp', axis=0,...  9.59 us
    dot_general x1, matrix products, add_projections(): query_acc = jnp.dot(normed, query_piece, preferred_element_type=jnp.float32)  9.19 us
  transfers between devices with their start and end apart: 5, of which 5 were waited for; matrix products, arithmetic and copies ran while one was open for 12% of the time, Pallas kernels for 0%

commit v1 on v0

--- a/solution.py
+++ b/solution.py
@@ -51,7 +51,12 @@
     )
     visible = jnp.arange(LEN)[None, :] < lengths[:, None]
     hidden = hidden_states
-    gathered = lax.all_gather(hidden, "mp", axis=1, tiled=True)
+    ring = [hidden]
+    for hop in range(3):
+        ring.append(lax.ppermute(ring[-1], "mp", [(dev, (dev + 1) % 4) for dev in range(4)]))
+    gathered = jnp.roll(
+        jnp.concatenate(ring[::-1], axis=1), (lax.axis_index("mp") + 1) * ring[0].shape[1], axis=1
+    )
     normed = normed_rows(gathered, norm_gain[0])
     zero_queries = jnp.zeros((tokens_here, inner_here), jnp.float32)
     zero_pairs = jnp.zeros((2, tokens_here, inner_here), jnp.float32)

time: 391 us -> 310 us (0.79)
  waiting for transfers between devices: 317 us -> 220 us
  local copies, waits for them, and re-layouts: 14.9 us -> 27.1 us
    all_gather x1 -> x0, waiting for transfers between devices: 77.4 us -> none  [local(): gathered = lax.all_gather(hidden, 'mp', axis=1, tiled=True)]
    ppermute x0 -> x3, waiting for transfers between devices: none -> 72.7 us  [local(): lax.ppermute(ring[-1], 'mp', [(dev, (dev + 1) % 4) for dev in range(4)])]
    all_gather x1, waiting for transfers between devices: 51.6 us -> 0.02 us  [local(): lax.all_gather(query_rows, 'dp', axis=0, tiled=True)]
    all_gather x1, waiting for transfers between devices: 80.9 us -> 43.1 us  [local(): lax.all_gather(pair_rows, 'dp', axis=0, tiled=True)]
    unnamed x17 -> x24, local copies, waits for them, and re-layouts: 3.56 us -> 12.3 us
  transfers between devices with their start and end apart: 5 -> 7, of which waited for: 5 -> 6; matrix products, arithmetic and copies ran while one was open for 12% -> 19% of each run, Pallas kernels for 0% -> 0%
where the time goes in v1:
time: 310 us
  waiting for transfers between devices  220 us (71%)
  matrix products  40.3 us (13%)
  local copies, waits for them, and re-layouts  27.1 us (9%)
  between operations  13.3 us (4%)
  other arithmetic  5.37 us (2%)
  starting transfers between devices  3.23 us (1%)
    reduce_scatter x1, waiting for transfers between devices, local(): lax.psum_scatter(partial_out.astype(jnp.bfloat16), 'mp', scatter_dimensio...  77 us
    ppermute x3, waiting for transfers between devices, local(): lax.ppermute(ring[-1], 'mp', [(dev, (dev + 1) % 4) for dev in range(4)])  72.7 us
    all_gather x1, waiting for transfers between devices, local(): lax.all_gather(pair_rows, 'dp', axis=0, tiled=True)  43.1 us
    all_gather x1, waiting for transfers between devices, local(): lax.all_gather(out_rows, 'dp', axis=0, tiled=True)  26.2 us
    dot_general x1, matrix products, add_projections(): jnp.einsum('td,dcf->ctf', normed, pair_piece, preferred_element_type=jnp....  13.7 us
    unnamed x24, local copies, waits for them, and re-layouts  12.3 us
    dot_general x1, matrix products, add_projections(): query_acc = jnp.dot(normed, query_piece, preferred_element_type=jnp.float32)  10.2 us
    dot_general x1, matrix products, local(): jnp.einsum('tf,df->td', attended, lax.all_gather(out_rows, 'dp', axis=0,...  9.6 us
  transfers between devices with their start and end apart: 7, of which 6 were waited for; matrix products, arithmetic and copies ran while one was open for 19% of the time, Pallas kernels for 0%

profile of v1, /device:TPU:0, one launch (start us, length us, event | category | flops | bytes accessed | tf_op | source)
XLA Modules:
  0.0 309.8 jit_solution(5803321465712935805)
XLA Ops:
  7.3 3.6 %copy.15 = bf16[1,512,2,1024]{3,1,2,0:T(8,128)(2,1)} copy(bf16[1,512,2,1024]{3,2,1,0:T(2,128)(2,1)} %param.11) | data formatting | bytes 4194304 | tf_op args[3]
  11.7 3.1 %collective-permute-start = (bf16[512,1024]{1,0:T(8,128)(2,1)S(1)}, bf16[512,1024]{1,0:T(8,128)(2,1)S(1)}, u32[]{:S(2)}, u32[]{:S(2)}) collective-permute-start(bf16[512,1024]{1,0:T(8,128)(2,1)S(1)} %copy-done.2), channel_id=1, source_target_pairs={{0,1},{1,2},{2,3},{3,0},{4,5},{5,6},{6,7},{7,4},{8,9},{9,10},{10,1... | collective-permute-start | bytes 3145736 | tf_op jit(solution)/shard_map/ppermute | solution.py:56
  14.8 25.2 %collective-permute-done = bf16[512,1024]{1,0:T(8,128)(2,1)S(1)} collective-permute-done((bf16[512,1024]{1,0:T(8,128)(2,1)S(1)}, bf16[512,1024]{1,0:T(8,128)(2,1)S(1)}, u32[]{:S(2)}, u32[]{:S(2)}) %collective-permute-start) | collective-permute-done | bytes 1048608 | tf_op jit(solution)/shard_map/ppermute | solution.py:56
  40.0 26.2 %collective-permute-done.1 = bf16[512,1024]{1,0:T(8,128)(2,1)} collective-permute-done((bf16[512,1024]{1,0:T(8,128)(2,1)S(1)}, bf16[512,1024]{1,0:T(8,128)(2,1)}, u32[]{:S(2)}, u32[]{:S(2)}) %collective-permute-start.1) | collective-permute-done | bytes 1048608 | tf_op jit(solution)/shard_map/ppermute | solution.py:56
  66.2 2.8 convolution_bitcast_fusion
  69.0 1.4 copy.21
  70.5 21.3 %collective-permute-done.2 = bf16[512,1024]{1,0:T(8,128)(2,1)} collective-permute-done((bf16[512,1024]{1,0:T(8,128)(2,1)}, bf16[512,1024]{1,0:T(8,128)(2,1)}, u32[]{:S(2)}, u32[]{:S(2)}) %collective-permute-start.2) | collective-permute-done | bytes 1048608 | tf_op jit(solution)/shard_map/ppermute | solution.py:56
  93.1 1.3 constant_dynamic-update-slice_fusion.6
  94.6 1.3 constant_dynamic-update-slice_fusion.3
  96.0 1.3 constant_dynamic-update-slice_fusion.2
  97.5 3.2 %copy-done.3 = bf16[512,8192]{1,0:T(8,128)(2,1)} copy-done((bf16[512,8192]{1,0:T(8,128)(2,1)}, bf16[512,8192]{1,0:T(8,128)(2,1)S(1)}, u32[]{:S(2)}) %copy-start.3) | copy-done | bytes 8388632
  101.6 10.2 %fusion.27 = bf16[512,1024]{1,0:T(8,128)(2,1)} fusion(bf16[1,4096,1024]{2,1,0:T(8,128)(2,1)} %all-gather.9.cloned.1.call-done, f32[4096]{0:T(1024)S(1)} %bitcast.40, f32[512]{0:T(512)S(1)} %add_rsqrt_fusion, bf16[512,8192]{1,0:T(8,128)(2,1)} %copy-done.3, s32[]{:T(128)S(6)} %select_n.18), kind=kOutput, calls=%fused_computation.28 | convolution fusion | flops 4303880192 | bytes 13649924 | tf_op jit(solution)/shard_map/dot_general | solution.py:37
  111.8 2.9 reshape.48
  114.8 43.1 %all-gather.7.cloned.1.call-done = bf16[1,4096,2,1024]{3,1,2,0:T(8,128)(2,1)} async-done(((bf16[1,512,2,1024]{3,1,2,0:T(8,128)(2,1)}), bf16[1,4096,2,1024]{3,1,2,0:T(8,128)(2,1)}) %all-gather.7.cloned.1.call-update) | async-done | bytes 16777232 | tf_op jit(solution)/shard_map/all_gather | solution.py:71
  157.9 13.7 %convert_bitcast_fusion = bf16[2,512,1024]{2,1,0:T(8,128)(2,1)S(1)} fusion(bf16[1,4096,2,1024]{3,1,2,0:T(8,128)(2,1)} %all-gather.7.cloned.1.call-done, f32[4096]{0:T(1024)S(1)} %bitcast.41, f32[512]{0:T(512)S(1)} %add_rsqrt_fusion, bf16[512,8192]{1,0:T(8,128)(2,1)} %copy-done.3, s32[]{:T(128)S(6)} %select_n.18), kind=kOutput, calls=%fused_computation.23 | convolution fusion | flops 8599371776 | bytes 23087108 | tf_op jit(solution)/shard_map/td,dcf->ctf/dot_general | solution.py:38
  171.6 1.5 fusion.44
  173.1 4.0 %reshape.49 = bf16[4,128,16,64]{3,2,1,0:T(8,128)(2,1)} reshape(bf16[1,512,1024]{2,1,0:T(8,128)(2,1)} %get-tuple-element.6) | data formatting | bytes 2097152 | tf_op jit(solution)/shard_map/convert_element_type | solution.py:74
  177.2 4.0 %reshape.47 = bf16[4,128,16,64]{3,2,1,0:T(8,128)(2,1)} reshape(bf16[1,512,1024]{2,1,0:T(8,128)(2,1)} %get-tuple-element.5) | data formatting | bytes 2097152 | tf_op jit(solution)/shard_map/convert_element_type | solution.py:75
  181.2 3.2 %fusion.15 = f32[4,16,128,128]{2,3,1,0:T(8,128)S(1)} fusion(bf16[4,128,16,64]{3,2,1,0:T(8,128)(2,1)} %reshape.49, bf16[4,128,16,64]{3,2,1,0:T(8,128)(2,1)S(1)} %reshape.48), kind=kOutput, calls=%fused_computation.18 | convolution fusion | flops 134217728 | bytes 6291456 | tf_op jit(solution)/shard_map/cqhe,ckhe->chqk/dot_general | solution.py:80
  184.4 1.8 fusion.45
  187.9 26.2 %all-gather.11.cloned.1.call-done = bf16[1,4096,1024]{2,1,0:T(8,128)(2,1)} async-done(((bf16[1,512,1024]{2,1,0:T(8,128)(2,1)}), bf16[1,4096,1024]{2,1,0:T(8,128)(2,1)}) %all-gather.11.cloned.1.call-update) | async-done | bytes 8388624 | tf_op jit(solution)/shard_map/all_gather | solution.py:92
  214.1 9.6 %fusion.10 = bf16[512,4096]{1,0:T(8,128)(2,1)} fusion(bf16[1,4096,1024]{2,1,0:T(8,128)(2,1)} %all-gather.11.cloned.1.call-done, bf16[128,8,4,128]{3,2,1,0:T(4,128)(2,1)S(1)} %bitcast.39), kind=kOutput, calls=%fused_computation.12 | convolution fusion | flops 4297064448 | bytes 13631488 | tf_op jit(solution)/shard_map/tf,df->td/dot_general | solution.py:89
  223.7 77.0 %reduce-scatter.2.cloned.1.call-done = bf16[512,1024]{1,0:T(8,128)(2,1)} async-done(((bf16[512,4096]{1,0:T(8,128)(2,1)}), bf16[512,1024]{1,0:T(8,128)(2,1)}) %reduce-scatter.2.cloned.1.call-update) | async-done | bytes 1048592 | tf_op jit(solution)/shard_map/reduce_scatter | solution.py:95
  300.7 2.6 add_convert_fusion
  (36 shorter events, 5.9 us)
Async XLA Ops:
  6.5 59.7 %copy-start = (f32[1,32,16]{1,2,0:T(8,128)S(1)}, f32[1,32,16]{1,2,0:T(8,128)}, u32[]{:S(2)}) copy-start(f32[1,32,16]{1,2,0:T(8,128)} %param.13) | copy-start | bytes 6148
  6.5 5.2 %copy-start.2 = (bf16[512,1024]{1,0:T(8,128)(2,1)S(1)}, bf16[512,1024]{1,0:T(8,128)(2,1)}, u32[]{:S(2)}) copy-start(bf16[512,1024]{1,0:T(8,128)(2,1)} %param.8) | copy-start | bytes 3145732
  6.5 95.1 %all-gather.9.cloned.1.call-start = ((), (), s32[]{:S(2)}) async-start(), calls=%async_computation.3 | async-start | bytes 9437184 | tf_op jit(solution)/shard_map/all_gather | solution.py:70
  7.3 150.6 %all-gather.7.cloned.1.call-start = ((), (), s32[]{:S(2)}) async-start(), calls=%async_computation.2 | async-start | bytes 18874368 | tf_op jit(solution)/shard_map/all_gather | solution.py:71
  10.9 59.5 %copy-start.7 = (s32[4]{0:T(128)S(1)}, s32[4]{0:T(128)}, u32[]{:S(2)}) copy-start(s32[4]{0:T(128)} %param.14) | copy-start | bytes 52
  10.9 203.2 %all-gather.11.cloned.1.call-start = ((), (), s32[]{:S(2)}) async-start(), calls=%async_computation.4 | async-start | bytes 9437184 | tf_op jit(solution)/shard_map/all_gather | solution.py:92
  11.7 289.0 %reduce-scatter.2.cloned.1.call-start = ((), (), s32[]{:S(2)}) async-start(), calls=%async_computation.1 | async-start | bytes 5242880 | tf_op jit(solution)/shard_map/reduce_scatter | solution.py:95
  11.7 28.3 %collective-permute-start = (bf16[512,1024]{1,0:T(8,128)(2,1)S(1)}, bf16[512,1024]{1,0:T(8,128)(2,1)S(1)}, u32[]{:S(2)}, u32[]{:S(2)}) collective-permute-start(bf16[512,1024]{1,0:T(8,128)(2,1)S(1)} %copy-done.2), channel_id=1, source_target_pairs={{0,1},{1,2},{2,3},{3,0},{4,5},{5,6},{6,7},{7,4},{8,9},{9,10},{10,1... | collective-permute-start | bytes 3145736 | tf_op jit(solution)/shard_map/ppermute | solution.py:56
  40.0 26.2 %collective-permute-start.1 = (bf16[512,1024]{1,0:T(8,128)(2,1)S(1)}, bf16[512,1024]{1,0:T(8,128)(2,1)}, u32[]{:S(2)}, u32[]{:S(2)}) collective-permute-start(bf16[512,1024]{1,0:T(8,128)(2,1)S(1)} %collective-permute-done), channel_id=1, source_target_pairs={{0,1},{1,2},{2,3},{3,0},{4,5},{5,6},{6,7},{7,4},{8,9},{9,10},{10,1... | collective-permute-start | bytes 3145736 | tf_op jit(solution)/shard_map/ppermute | solution.py:56
  66.2 25.6 %collective-permute-start.2 = (bf16[512,1024]{1,0:T(8,128)(2,1)}, bf16[512,1024]{1,0:T(8,128)(2,1)}, u32[]{:S(2)}, u32[]{:S(2)}) collective-permute-start(bf16[512,1024]{1,0:T(8,128)(2,1)} %collective-permute-done.1), channel_id=1, source_target_pairs={{0,1},{1,2},{2,3},{3,0},{4,5},{5,6},{6,7},{7,4},{8,9},{9,10},{10,1... | collective-permute-start | bytes 3145736 | tf_op jit(solution)/shard_map/ppermute | solution.py:56
  97.3 4.3 %copy-start.6 = (f32[1,4096]{1,0:T(1,128)S(1)}, f32[1,4096]{1,0:T(1,128)}, u32[]{:S(2)}) copy-start(f32[1,4096]{1,0:T(1,128)} %param.9) | copy-start | bytes 49156
  97.5 3.2 %copy-start.3 = (bf16[512,8192]{1,0:T(8,128)(2,1)}, bf16[512,8192]{1,0:T(8,128)(2,1)S(1)}, u32[]{:S(2)}) copy-start(bf16[512,8192]{1,0:T(8,128)(2,1)S(1)} %constant_dynamic-update-slice_fusion) | copy-start | bytes 25165828
  181.2 3.3 %copy-start.5 = (f32[16,128,128]{1,2,0:T(8,128)S(1)}, f32[16,128,128]{1,2,0:T(8,128)}, u32[]{:S(2)}) copy-start(f32[16,128,128]{1,2,0:T(8,128)} %copy.21) | copy-start | bytes 3145732
  184.4 1.8 copy-start.4
  214.1 89.2 %copy-start.1 = (f32[1,32,16]{1,2,0:T(8,128)S(1)}, f32[1,32,16]{1,2,0:T(8,128)}, u32[]{:S(2)}) copy-start(f32[1,32,16]{1,2,0:T(8,128)} %param.13) | copy-start | bytes 6148
Sparse Core Ops, SparseCore 0:
  9.2 56.9 all-gather.8
  68.1 89.7 all-gather.6
  159.8 54.2 all-gather.10
  223.8 76.7 reduce-scatter.1
